TPU v7x, 32 devices: a whole 2x2x4 slice. The times are simulated.
32 devices in a mesh: dp: 4 (over z), group: 8 (over y, x, core).
Axes of the slice: x: 2, y: 2, z: 4, core: 2. Of those that a mesh axis runs over, the one named last changes fastest.
Arguments:
- tokens: bfloat16 [128, 160, 768], P(('dp', 'group')), may hold values from -6 to 6
- cotangent: bfloat16 [128, 160, 768], P(('dp', 'group')), may hold values from -6 to 6
- counts: int32 [128], P(('dp', 'group')), may hold values from 96 to 160, as said below
- first_gain: float32 [768], replicated, may hold values from 0.5 to 1.5
- first_shift: float32 [768], replicated, may hold values from -1.75 to 1.75
- joined_weight: bfloat16 [768, 2304], replicated, may hold values from -0.21875 to 0.21875
- joined_bias: float32 [2, 768], replicated, may hold values from -1.75 to 1.75
- merge_weight: bfloat16 [768, 768], replicated, may hold values from -0.75 to 0.75
- merge_bias: float32 [768], replicated, may hold values from -1.75 to 1.75
- second_gain: float32 [768], replicated, may hold values from 0.5 to 1.5
- second_shift: float32 [768], replicated, may hold values from -1.75 to 1.75
- up_weight: bfloat16 [768, 3072], replicated, may hold values from -0.21875 to 0.21875
- up_bias: float32 [3072], replicated, may hold values from -1.75 to 1.75
- down_weight: bfloat16 [3072, 768], replicated, may hold values from -0.109375 to 0.109375
- down_bias: float32 [768], replicated, may hold values from -1.75 to 1.75
Outputs:
- result: bfloat16 [128, 160, 768], P(('dp', 'group'))
- token_grad: bfloat16 [128, 160, 768], P(('dp', 'group'))
- first_gain_grad: float32 [768], replicated
- first_shift_grad: float32 [768], replicated
- joined_weight_grad: float32 [768, 2304], replicated
- joined_bias_grad: float32 [2, 768], replicated
- merge_weight_grad: float32 [768, 768], replicated
- merge_bias_grad: float32 [768], replicated
- second_gain_grad: float32 [768], replicated
- second_shift_grad: float32 [768], replicated
- up_weight_grad: float32 [768, 3072], replicated
- up_bias_grad: float32 [3072], replicated
- down_weight_grad: float32 [3072, 768], replicated
- down_bias_grad: float32 [768], replicated
Inputs may be any that keep to these rules, and one draw needn't show every extreme that they name: `counts`: item j of a device is owned by the device with index j // 1 along dp and the same index along group; the items owned by one device hold 512 visible patches together.
All inputs are finite; a program needn't handle non-finite values.
Results may differ from a plain program's by a relative error of at most 0.012.
Values may be sent and summed in bfloat16 or wider, within the bound.
No kernel may reach another device: no remote copies, remote signals or barrier semaphores. Data moves between devices by JAX's collectives and lax.ppermute only.
A program may use at most 256 MiB of HBM per device.

v0:
```python
import jax
import jax.numpy as jnp
from jax import lax
from jax.sharding import PartitionSpec as P

HEADS = 12
HEAD_DIM = 64
VIS_MEAN = 128
EPS = 1e-06
NEG = -1e30


def norm_rows(matrix, gain_row, shift_row):
    row_mean = jnp.mean(matrix, axis=-1, keepdims=True)
    centred = matrix - row_mean
    variance = jnp.mean(centred * centred, axis=-1, keepdims=True)
    return centred * lax.rsqrt(variance + EPS) * gain_row + shift_row


def exact_gelu(matrix):
    return jax.nn.gelu(matrix, approximate=False)


def rows_inner(left, right):
    return lax.dot_general(
        left, right, (((0,), (0,)), ((), ())), preferred_element_type=jnp.float32
    )


def rows_back(left, right):
    return lax.dot_general(
        left, right, (((1,), (1,)), ((), ())), preferred_element_type=jnp.float32
    )


def attend(queries, key_rows, values, allowed):
    factor = HEAD_DIM ** (-0.5)
    scores = (
        jnp.einsum("qhd,khd->hqk", queries, key_rows, preferred_element_type=jnp.float32) * factor
    )
    scores = jnp.where(allowed[None], scores, NEG)
    highest = jnp.max(scores, axis=-1, keepdims=True)
    raised = jnp.exp(scores - highest)
    row_total = jnp.sum(raised, axis=-1, keepdims=True)
    probs_low = (raised / row_total).astype(jnp.bfloat16)
    mixture = jnp.einsum("hqk,khd->qhd", probs_low, values, preferred_element_type=jnp.float32)
    return (mixture, highest[..., 0] + jnp.log(row_total[..., 0]))


def attend_back(queries, key_rows, values, allowed, logsum, grad_mixture):
    factor = HEAD_DIM ** (-0.5)
    scores = (
        jnp.einsum("qhd,khd->hqk", queries, key_rows, preferred_element_type=jnp.float32) * factor
    )
    scores = jnp.where(allowed[None], scores, NEG)
    soft = jnp.exp(scores - logsum[..., None])
    soft_low = soft.astype(jnp.bfloat16)
    grad_probs = jnp.einsum(
        "qhd,khd->hqk", grad_mixture, values, preferred_element_type=jnp.float32
    )
    grad_scores = soft * (grad_probs - jnp.sum(soft * grad_probs, axis=-1, keepdims=True))
    grad_low = grad_scores.astype(jnp.bfloat16)
    grad_queries = (
        jnp.einsum("hqk,khd->qhd", grad_low, key_rows, preferred_element_type=jnp.float32) * factor
    )
    grad_keys = (
        jnp.einsum("hqk,qhd->khd", grad_low, queries, preferred_element_type=jnp.float32) * factor
    )
    grad_values = jnp.einsum(
        "hqk,qhd->khd", soft_low, grad_mixture, preferred_element_type=jnp.float32
    )
    return (grad_queries, grad_keys, grad_values)


def layer(packed, cot_rows, visible, weights, attention, attention_back, settle_mlp):
    (
        first_gain,
        first_shift,
        joined_weight,
        joined_bias,
        merge_weight,
        merge_bias,
        second_gain,
        second_shift,
        up_weight,
        up_bias,
        down_weight,
        down_bias,
    ) = weights
    row_count, features = packed.shape
    inputs = packed.astype(jnp.float32)
    normed, first_back = jax.vjp(norm_rows, inputs, first_gain, first_shift)
    normed_low = normed.astype(jnp.bfloat16)
    bias_full = jnp.concatenate(
        [joined_bias[0], jnp.zeros((features,), jnp.float32), joined_bias[1]]
    )
    joined = jnp.dot(normed_low, joined_weight, preferred_element_type=jnp.float32) + bias_full
    joined_low = joined.astype(jnp.bfloat16).reshape(row_count, 3, HEADS, HEAD_DIM)
    queries = joined_low[:, 0]
    key_rows = joined_low[:, 1]
    values = joined_low[:, 2]
    mixture, kept_stats = attention(queries, key_rows, values)
    mixture_low = mixture.reshape(row_count, features).astype(jnp.bfloat16)
    middle = (
        inputs + jnp.dot(mixture_low, merge_weight, preferred_element_type=jnp.float32) + merge_bias
    )
    second, second_back = jax.vjp(norm_rows, middle, second_gain, second_shift)
    second_low = second.astype(jnp.bfloat16)
    hidden = jnp.dot(second_low, up_weight, preferred_element_type=jnp.float32) + up_bias
    active, gelu_back = jax.vjp(exact_gelu, hidden)
    active_low = active.astype(jnp.bfloat16)
    outer = jnp.dot(active_low, down_weight, preferred_element_type=jnp.float32) + down_bias
    result = ((middle + outer) * visible[:, None]).astype(jnp.bfloat16)
    grad_result = cot_rows.astype(jnp.float32) * visible[:, None]
    grad_out = grad_result.astype(jnp.bfloat16)
    grad_down = rows_inner(active_low, grad_out)
    grad_down_bias = jnp.sum(grad_out.astype(jnp.float32), axis=0)
    (grad_active,) = gelu_back(rows_back(grad_out, down_weight))
    grad_hidden = grad_active.astype(jnp.bfloat16)
    grad_up = rows_inner(second_low, grad_hidden)
    grad_up_bias = jnp.sum(grad_hidden.astype(jnp.float32), axis=0)
    grad_middle, grad_second_gain, grad_second_shift = second_back(
        rows_back(grad_hidden, up_weight)
    )
    grad_middle = grad_middle + grad_result
    mlp_sums = settle_mlp(
        (grad_second_gain, grad_second_shift, grad_up, grad_up_bias, grad_down, grad_down_bias)
    )
    grad_branch = grad_middle.astype(jnp.bfloat16)
    grad_merge = rows_inner(mixture_low, grad_branch)
    grad_merge_bias = jnp.sum(grad_branch.astype(jnp.float32), axis=0)
    grad_mixture = (
        rows_back(grad_branch, merge_weight)
        .astype(jnp.bfloat16)
        .reshape(row_count, HEADS, HEAD_DIM)
    )
    grad_queries, grad_keys, grad_values = attention_back(
        queries, key_rows, values, kept_stats, grad_mixture
    )
    grad_joined = jnp.stack([grad_queries, grad_keys, grad_values], axis=1)
    grad_joined = grad_joined.reshape(row_count, 3 * features).astype(jnp.bfloat16)
    grad_joined_weight = rows_inner(normed_low, grad_joined)
    joined_sums = jnp.sum(grad_joined.astype(jnp.float32), axis=0)
    grad_joined_bias = jnp.stack([joined_sums[:features], joined_sums[2 * features :]])
    grad_inputs, grad_first_gain, grad_first_shift = first_back(
        rows_back(grad_joined, joined_weight)
    )
    grad_rows = (grad_middle + grad_inputs).astype(jnp.bfloat16)
    attn_grads = (
        grad_first_gain,
        grad_first_shift,
        grad_joined_weight,
        grad_joined_bias,
        grad_merge,
        grad_merge_bias,
    )
    return (result, grad_rows, attn_grads, mlp_sums)


def shards(
    tokens,
    cotangent,
    counts,
    first_gain,
    first_shift,
    joined_weight,
    joined_bias,
    merge_weight,
    merge_bias,
    second_gain,
    second_shift,
    up_weight,
    up_bias,
    down_weight,
    down_bias,
):
    weights = (
        first_gain,
        first_shift,
        joined_weight,
        joined_bias,
        merge_weight,
        merge_bias,
        second_gain,
        second_shift,
        up_weight,
        up_bias,
        down_weight,
        down_bias,
    )
    item_count, slot_count, features = tokens.shape
    slot_range = jnp.arange(slot_count, dtype=jnp.int32)

    def settle_mlp(parts):
        return parts

    arrived_all = (
        lax.all_to_all(tokens, "dp", split_axis=0, concat_axis=0, tiled=True),
        lax.all_to_all(cotangent, "dp", split_axis=0, concat_axis=0, tiled=True),
        lax.all_to_all(counts.astype(jnp.bfloat16), "dp", split_axis=0, concat_axis=0, tiled=True),
    )
    arrived, arrived_cot, arrived_counts = arrived_all
    arrived_counts = arrived_counts.astype(jnp.int32)
    row_ends = jnp.cumsum(arrived_counts)
    starts = row_ends - arrived_counts
    total_rows = item_count * VIS_MEAN
    position = jnp.arange(total_rows, dtype=jnp.int32)
    segment = jnp.sum((position[:, None] >= row_ends[None, :]).astype(jnp.int32), axis=1)
    member = segment[:, None] == jnp.arange(item_count, dtype=jnp.int32)[None, :]
    offset = position - jnp.sum(jnp.where(member, starts[None, :], 0), axis=1)
    source = segment * slot_count + offset
    packed = arrived.reshape(-1, features)[source]
    cot_rows = arrived_cot.reshape(-1, features)[source]
    visible = jnp.ones((total_rows,), jnp.float32)
    block = 512
    count_blocks = total_rows // block
    window = min(total_rows, (block + 2 * slot_count + 127) // 128 * 128)
    block_ids = jnp.arange(count_blocks, dtype=jnp.int32)

    def window_start(index):
        return jnp.clip(index * block - slot_count, 0, total_rows - window)

    def attention(queries, key_rows, values):

        def forward_block(pieces):
            query_block, segment_block, index = pieces
            begin = window_start(index)
            near_keys = lax.dynamic_slice_in_dim(key_rows, begin, window, 0)
            near_values = lax.dynamic_slice_in_dim(values, begin, window, 0)
            near_segment = lax.dynamic_slice_in_dim(segment, begin, window, 0)
            allowed = segment_block[:, None] == near_segment[None, :]
            return attend(query_block, near_keys, near_values, allowed)

        mixture, logsum = lax.map(
            forward_block,
            (
                queries.reshape(count_blocks, block, HEADS, HEAD_DIM),
                segment.reshape(count_blocks, block),
                block_ids,
            ),
        )
        return (mixture.reshape(total_rows, HEADS, HEAD_DIM), logsum)

    def attention_back(queries, key_rows, values, logsum, grad_mixture):

        def back_block(carry, pieces):
            query_block, segment_block, logsum_block, grad_block, index = pieces
            begin = window_start(index)
            near_keys = lax.dynamic_slice_in_dim(key_rows, begin, window, 0)
            near_values = lax.dynamic_slice_in_dim(values, begin, window, 0)
            near_segment = lax.dynamic_slice_in_dim(segment, begin, window, 0)
            allowed = segment_block[:, None] == near_segment[None, :]
            grad_queries, grad_keys, grad_values = attend_back(
                query_block, near_keys, near_values, allowed, logsum_block, grad_block
            )
            key_total = lax.dynamic_update_slice_in_dim(
                carry[0], lax.dynamic_slice_in_dim(carry[0], begin, window, 0) + grad_keys, begin, 0
            )
            value_total = lax.dynamic_update_slice_in_dim(
                carry[1],
                lax.dynamic_slice_in_dim(carry[1], begin, window, 0) + grad_values,
                begin,
                0,
            )
            return ((key_total, value_total), grad_queries)

        zeroed = jnp.zeros((total_rows, HEADS, HEAD_DIM), jnp.float32)
        (grad_keys, grad_values), grad_queries = lax.scan(
            back_block,
            (zeroed, zeroed),
            (
                queries.reshape(count_blocks, block, HEADS, HEAD_DIM),
                segment.reshape(count_blocks, block),
                logsum,
                grad_mixture.reshape(count_blocks, block, HEADS, HEAD_DIM),
                block_ids,
            ),
        )
        return (grad_queries.reshape(total_rows, HEADS, HEAD_DIM), grad_keys, grad_values)

    out_rows, grad_rows, attn_grads, mlp_sums = layer(
        packed, cot_rows, visible, weights, attention, attention_back, settle_mlp
    )
    slot_index = starts[:, None] + slot_range[None, :]
    inside = slot_range[None, :] < arrived_counts[:, None]
    picked = jnp.minimum(slot_index, total_rows - 1)
    back_out = jnp.where(inside[..., None], out_rows[picked], jnp.zeros((), jnp.bfloat16))
    back_grad = jnp.where(inside[..., None], grad_rows[picked], jnp.zeros((), jnp.bfloat16))
    returned = (
        lax.all_to_all(back_out, "dp", split_axis=0, concat_axis=0, tiled=True),
        lax.all_to_all(back_grad, "dp", split_axis=0, concat_axis=0, tiled=True),
    )
    result = returned[0]
    token_grad = returned[1]
    summed = lax.psum(attn_grads + mlp_sums, ("dp", "group"))
    return (
        result,
        token_grad,
        summed[0],
        summed[1],
        summed[2],
        summed[3],
        summed[4],
        summed[5],
        summed[6],
        summed[7],
        summed[8],
        summed[9],
        summed[10],
        summed[11],
    )


def solution(mesh):
    in_specs = (
        P(("dp", "group"), None, None),
        P(("dp", "group"), None, None),
        P(("dp", "group")),
        P(),
        P(),
        P(),
        P(),
        P(),
        P(),
        P(),
        P(),
        P(),
        P(),
        P(),
        P(),
    )
    out_specs = (
        P(("dp", "group"), None, None),
        P(("dp", "group"), None, None),
        P(),
        P(),
        P(),
        P(),
        P(),
        P(),
        P(),
        P(),
        P(),
        P(),
        P(),
        P(),
    )
    return jax.shard_map(shards, mesh=mesh, in_specs=in_specs, out_specs=out_specs, check_vma=False)
```

profile of v0, /device:TPU:0, one launch (start us, length us, event | category | flops | bytes accessed | tf_op | source)
XLA Modules:
  0.0 690.3 jit_solution(2284785976258960198)
XLA Ops:
  8.1 11.8 %all_to_all.29 = bf16[4,1,1]{2,1,0:T(2,128)(2,1)S(1)} all-to-all(bf16[4,1,1]{2,1,0:T(2,128)(2,1)S(1)} %copy.58), channel_id=1, replica_groups=mesh['dp'=4,'group'=8] {'dp'}, dimensions={0} | all-to-all | bytes 16 | tf_op jit(solution)/shard_map/all_to_all | solution.py:200
  19.9 4.2 all-to-all-start.1
  27.4 19.9 %all-to-all-done.1 = bf16[4,160,768]{2,1,0:T(8,128)(2,1)} async-done(((bf16[4,160,768]{2,1,0:T(8,128)(2,1)}), bf16[4,160,768]{2,1,0:T(8,128)(2,1)}, u32[]{:S(2)}, u32[]{:S(2)}) %all-to-all-start.1) | async-done | bytes 983072 | tf_op jit(solution)/shard_map/all_to_all | solution.py:198
  47.4 4.3 all-to-all-start.3
  51.7 4.4 gather_fusion
  60.1 4.7 fusion.12
  64.8 4.3 copy.59
  69.1 3.5 fusion.13
  72.6 3.7 fusion
  77.2 5.5 fusion.29
  82.6 4.9 gather_fusion.2
  90.6 5.5 fusion.44
  96.2 19.0 %convert_reduce_fusion = (f32[3072]{0:T(1024)}, bf16[512,3072]{1,0:T(8,128)(2,1)S(1)}, f32[512,3072]{1,0:T(8,128)}) fusion(f32[512,3072]{1,0:T(8,128)S(1)} %fusion.44, f32[3072]{0:T(1024)S(1)} %copy-done.31, bf16[512,768]{1,0:T(8,128)(2,1)S(1)} %copy-done.7, bf16[3072,768]{1,0:T(8,128)(2,1)S(1)} %bitcast.103), kind=kOutput, calls=%fused_computation.15 | convolution fusion | flops 2533880832 | bytes 21258240 | tf_op jit(solution)/shard_map/dot_general | solution.py:31
  115.2 3.5 multiply_reduce_fusion.1
  126.4 9.0 %fusion.26 = bf16[512,1,12,64]{0,3,2,1:T(8,128)(2,1)} fusion(bf16[512,12,64]{0,2,1:T(8,128)(2,1)} %bitcast.89, f32[12,512]{1,0:T(8,128)} %log_add_fusion, f32[12,512,512]{1,2,0:T(8,128)} %copy-done.1, pred[512,512]{0,1:T(8,128)(4,1)} %broadcast_compare_fusion), kind=kOutput, calls=%fused_computation.66 | convolution fusion | flops 415236096 | bytes 14442496 | tf_op jit(solution)/shard_map/while/body/eval_jaxpr/hqk,qhd->khd/dot_general | solution.py:69
  135.4 9.9 %multiply_reduce_fusion = (f32[12,512]{1,0:T(8,128)S(1)}, f32[12,512,512]{1,2,0:T(8,128)}) fusion(f32[12,512]{1,0:T(8,128)S(1)} %copy-done.21, f32[12,512,512]{1,2,0:T(8,128)} %copy-done.1, pred[512,512]{0,1:T(8,128)(4,1)S(1)} %copy-done.10, bf16[512,12,64]{0,2,1:T(8,128)(2,1)S(1)} %bitcast.90, bf16[512,3,12,64]{0,3,2,1:T(8,128)(2,1)} %bitcast.78), kind=kOutput, calls=%fused_computation.5 | convolution fusion | flops 418375680 | bytes 27049984 | tf_op jit(solution)/shard_map/while/body/eval_jaxpr/qhd,khd->hqk/dot_general | solution.py:58
  145.4 7.1 %multiply_convert_fusion = bf16[12,512,512]{1,2,0:T(8,128)(2,1)S(1)} fusion(f32[12,512,512]{1,2,0:T(8,128)} %get-tuple-element.113, f32[12,512]{1,0:T(8,128)S(1)} %get-tuple-element.112, f32[12,512]{1,0:T(8,128)S(1)} %copy-done.21, f32[12,512,512]{1,2,0:T(8,128)S(1)} %bitcast.75, pred[512,512]{0,1:T(8,128)(4,1)S(1)} %copy-done.10), kind=kLoop, calls=%fused_computation.4 | loop fusion | flops 18874368 | bytes 31768576 | tf_op jit(solution)/shard_map/while/body/eval_jaxpr/convert_element_type | solution.py:62
  159.8 5.6 fusion.43
  167.0 3.8 convert_reduce_fusion.1
  170.9 5.3 fusion.39
  176.2 5.4 fusion.52
  185.0 4.9 fusion.45
  193.5 5.2 gather_fusion.3
  198.7 7.3 %add_convert_fusion.2 = bf16[512,768]{1,0:T(8,128)(2,1)} fusion(f32[512,768]{1,0:T(8,128)} %copy-done.11, bf16[512,3072]{1,0:T(8,128)(2,1)} %copy-done.17, bf16[3072,768]{1,0:T(8,128)(2,1)} %param.28, f32[768]{0:T(1024)S(1)} %copy-done.44), kind=kOutput, calls=%fused_computation.63 | convolution fusion | flops 2417098752 | bytes 10226688 | tf_op jit(solution)/shard_map/dot_general | solution.py:112
  206.0 5.2 gather_fusion.1
  213.9 40.4 %all_to_all.30 = bf16[4,160,768]{2,1,0:T(8,128)(2,1)} all-to-all(bf16[4,160,768]{2,1,0:T(8,128)(2,1)S(1)} %get-tuple-element.106), channel_id=1, replica_groups=mesh['dp'=4,'group'=8] {'dp'}, dimensions={0} | all-to-all | bytes 1966080 | tf_op jit(solution)/shard_map/all_to_all | solution.py:290
  254.3 4.2 all-to-all-start.4
  260.7 54.2 %all-reduce = (f32[768]{0:T(1024)}, f32[768]{0:T(1024)}, f32[2,768]{1,0:T(2,128)}, f32[768]{0:T(1024)}, f32[768]{0:T(1024)}, /*index=5*/f32[768]{0:T(1024)}, f32[3072]{0:T(1024)}, f32[768]{0:T(1024)}) all-reduce(f32[768]{0:T(1024)} %get-tuple-element.62, ...), channel_id=1, replica_groups=mesh['dp'=4,'group'=8] {'dp','group'}, use_global_device_ids=true, to_apply=%region_15.16 | all-reduce | flops 9216 | bytes 73728 | tf_op jit(solution)/shard_map/psum | solution.py:295
  314.9 342.7 %all-reduce.4.cloned.1.call-done = (f32[768,2304]{1,0:T(8,128)}, f32[768,768]{1,0:T(8,128)}, f32[768,3072]{1,0:T(8,128)}, f32[3072,768]{1,0:T(8,128)}) async-done(((f32[768,2304]{1,0:T(8,128)}, f32[768,768]{1,0:T(8,128)}, f32[768,3072]{1,0:T(8,128)}, f32[3072,768]{1,0:T(8,128)}), (f32[768,2304]{1,0:T(8,128)}, f32[768,768]{1,0:T(8,128)}, f32[768,3072]{1,0:T(8,128)}, ...) | async-done | bytes 28311568 | tf_op jit(solution)/shard_map/psum | solution.py:295
  662.1 6.6 copy.77
  670.0 9.3 %copy.79 = f32[768,3072]{1,0:T(8,128)} copy(f32[768,3072]{1,0:T(8,128)} %get-tuple-element.139) | data formatting | bytes 18874368
  679.4 3.7 copy.80
  (181 shorter events, 46.2 us)
Async XLA Ops:
  7.2 52.9 %copy-start = (bf16[768,2304]{1,0:T(8,128)(2,1)S(1)}, bf16[768,2304]{1,0:T(8,128)(2,1)}, u32[]{:S(2)}) copy-start(bf16[768,2304]{1,0:T(8,128)(2,1)} %param.20) | copy-start | bytes 10616836
  19.9 27.5 %all-to-all-start.1 = ((bf16[4,160,768]{2,1,0:T(8,128)(2,1)}), bf16[4,160,768]{2,1,0:T(8,128)(2,1)}, u32[]{:S(2)}, u32[]{:S(2)}) async-start(bf16[4,160,768]{2,1,0:T(8,128)(2,1)} %param.15), calls=%async_computation.1 | async-start | bytes 1966080 | tf_op jit(solution)/shard_map/all_to_all | solution.py:198
  47.4 35.3 %all-to-all-start.3 = ((bf16[4,160,768]{2,1,0:T(8,128)(2,1)}), bf16[4,160,768]{2,1,0:T(8,128)(2,1)}, u32[]{:S(2)}, u32[]{:S(2)}) async-start(bf16[4,160,768]{2,1,0:T(8,128)(2,1)} %param.16), calls=%async_computation.3 | async-start | bytes 1966080 | tf_op jit(solution)/shard_map/all_to_all | solution.py:199
  51.6 8.5 %copy-start.28 = (f32[768]{0:T(1024)S(1)}, f32[768]{0:T(1024)}, u32[]{:S(2)}) copy-start(f32[768]{0:T(1024)} %param.18) | copy-start | bytes 9220
  51.6 8.5 %copy-start.42 = (f32[768]{0:T(1024)S(1)}, f32[768]{0:T(1024)}, u32[]{:S(2)}) copy-start(f32[768]{0:T(1024)} %param.19) | copy-start | bytes 9220
  51.7 606.0 %all-reduce.4.cloned.1.call-start = ((), (), s32[]{:S(2)}) async-start(), calls=%async_computation.5 | async-start | bytes 56623104 | tf_op jit(solution)/shard_map/psum | solution.py:295
  90.2 28.6 %copy-start.11 = (f32[512,768]{1,0:T(8,128)}, f32[512,768]{1,0:T(8,128)S(1)}, u32[]{:S(2)}) copy-start(f32[512,768]{1,0:T(8,128)S(1)} %get-tuple-element.110) | copy-start | bytes 4718596
  90.2 5.9 slice-start.12
  90.6 5.6 copy-start.7
  90.6 24.6 %slice-start.10 = ((s8[4718592]{0:T(1024)(128)(4,1)}), s8[4194304]{0:T(1024)(128)(4,1)S(1)}, s32[]{:S(2)}) async-start(s8[4718592]{0:T(1024)(128)(4,1)} %bitcast.100), calls=%async_computation.16 | async-start | bytes 8388608
  96.2 19.0 %copy-start.13 = (f32[512,3072]{1,0:T(8,128)}, f32[512,3072]{1,0:T(8,128)S(1)}, u32[]{:S(2)}) copy-start(f32[512,3072]{1,0:T(8,128)S(1)} %fusion.44) | copy-start | bytes 18874372
  96.2 19.0 %slice-start.11 = ((s8[4718592]{0:T(1024)(128)(4,1)}), s8[524288]{0:T(1024)(128)(4,1)S(1)}, s32[]{:S(2)}) async-start(s8[4718592]{0:T(1024)(128)(4,1)} %bitcast.100), calls=%async_computation.17 | async-start | bytes 1048576
  126.4 9.0 %copy-start.10 = (pred[512,512]{0,1:T(8,128)(4,1)S(1)}, pred[512,512]{0,1:T(8,128)(4,1)}, u32[]{:S(2)}) copy-start(pred[512,512]{0,1:T(8,128)(4,1)} %broadcast_compare_fusion) | copy-start | bytes 786436
  126.4 9.0 %copy-start.14 = (bf16[512,768]{0,1:T(8,128)(2,1)S(1)}, bf16[512,768]{0,1:T(8,128)(2,1)}, u32[]{:S(2)}) copy-start(bf16[512,768]{0,1:T(8,128)(2,1)} %copy.61) | copy-start | bytes 2359300
  126.4 9.0 %copy-start.21 = (f32[12,512]{1,0:T(8,128)S(1)}, f32[12,512]{1,0:T(8,128)}, u32[]{:S(2)}) copy-start(f32[12,512]{1,0:T(8,128)} %log_add_fusion) | copy-start | bytes 73732
  126.4 18.9 %slice-start = ((s8[12582912]{0:T(1024)(128)(4,1)}), s8[4194304]{0:T(1024)(128)(4,1)S(1)}, s32[]{:S(2)}) async-start(s8[12582912]{0:T(1024)(128)(4,1)} %bitcast.74), calls=%async_computation.6 | async-start | bytes 8388608
  126.4 18.9 %slice-start.1 = ((s8[12582912]{0:T(1024)(128)(4,1)}), s8[4194304]{0:T(1024)(128)(4,1)S(1)}, s32[]{:S(2)}) async-start(s8[12582912]{0:T(1024)(128)(4,1)} %bitcast.74), calls=%async_computation.7 | async-start | bytes 8388608
  135.4 9.9 %slice-start.2 = ((s8[12582912]{0:T(1024)(128)(4,1)}), s8[4194304]{0:T(1024)(128)(4,1)S(1)}, s32[]{:S(2)}) async-start(s8[12582912]{0:T(1024)(128)(4,1)} %bitcast.74), calls=%async_computation.8 | async-start | bytes 8388608
  145.4 7.2 %copy-start.2 = (bf16[512,2304]{0,1:T(8,128)(2,1)S(1)}, bf16[512,2304]{0,1:T(8,128)(2,1)}, u32[]{:S(2)}) copy-start(bf16[512,2304]{0,1:T(8,128)(2,1)} %copy.59) | copy-start | bytes 7077892
  157.5 7.9 %slice-start.6 = ((s8[6291456]{0:T(1024)(128)(4,1)}), s8[4194304]{0:T(1024)(128)(4,1)S(1)}, s32[]{:S(2)}) async-start(s8[6291456]{0:T(1024)(128)(4,1)} %bitcast.83), calls=%async_computation.12 | async-start | bytes 8388608
  157.5 7.9 %slice-start.8 = ((s8[6291456]{0:T(1024)(128)(4,1)}), s8[4194304]{0:T(1024)(128)(4,1)S(1)}, s32[]{:S(2)}) async-start(s8[6291456]{0:T(1024)(128)(4,1)} %bitcast.85), calls=%async_computation.14 | async-start | bytes 8388608
  159.7 5.6 slice-start.7
  159.8 5.6 slice-start.9
  159.8 5.6 copy-start.32
  167.0 9.2 %copy-start.17 = (bf16[512,3072]{1,0:T(8,128)(2,1)}, bf16[512,3072]{1,0:T(8,128)(2,1)S(1)}, u32[]{:S(2)}) copy-start(bf16[512,3072]{1,0:T(8,128)(2,1)S(1)} %multiply_convert_fusion.1) | copy-start | bytes 9437188
  185.0 6.2 copy-start.6
  185.0 6.2 copy-start.9
  254.3 60.6 %all-to-all-start.4 = ((bf16[4,160,768]{2,1,0:T(8,128)(2,1)}), bf16[4,160,768]{2,1,0:T(8,128)(2,1)}, u32[]{:S(2)}, u32[]{:S(2)}) async-start(bf16[4,160,768]{2,1,0:T(8,128)(2,1)} %get-tuple-element.105), calls=%async_computation.4 | async-start | bytes 1966080 | tf_op jit(solution)/shard_map/all_to_all | solution.py:291
  662.1 6.6 copy-start.18
  668.6 10.7 %slice-start.3 = ((s8[9437184]{0:T(1024)(128)(4,1)}), s8[4194304]{0:T(1024)(128)(4,1)S(1)}, s32[]{:S(2)}) async-start(s8[9437184]{0:T(1024)(128)(4,1)} %bitcast.81), calls=%async_computation.9 | async-start | bytes 8388608
  670.0 9.3 %slice-start.4 = ((s8[9437184]{0:T(1024)(128)(4,1)}), s8[4194304]{0:T(1024)(128)(4,1)S(1)}, s32[]{:S(2)}) async-start(s8[9437184]{0:T(1024)(128)(4,1)} %bitcast.81), calls=%async_computation.10 | async-start | bytes 8388608
  670.0 9.3 %slice-start.5 = ((s8[9437184]{0:T(1024)(128)(4,1)}), s8[1048576]{0:T(1024)(128)(4,1)S(1)}, s32[]{:S(2)}) async-start(s8[9437184]{0:T(1024)(128)(4,1)} %bitcast.81), calls=%async_computation.11 | async-start | bytes 2097152
  (33 other events, 116.6 us)
Sparse Core Ops, SparseCore 0:
  181.7 475.8 all-reduce.3
where the time goes:
time: 700 us; the launch traced here: 690 us
  waiting for transfers between devices  363 us (52%)
  blocking collectives  106 us (15%)
  matrix products  101 us (14%)
  local copies, waits for them, and re-layouts  58.6 us (8%)
  other arithmetic  34.2 us (5%)
  between operations  15.1 us (2%)
  starting transfers between devices  12.8 us (2%)
    psum x1, waiting for transfers between devices, shards(): summed = lax.psum(attn_grads + mlp_sums, ('dp', 'group'))  343 us
    psum x1, blocking collectives, shards(): summed = lax.psum(attn_grads + mlp_sums, ('dp', 'group'))  54.2 us
    all_to_all x1, blocking collectives, shards(): lax.all_to_all(back_out, 'dp', split_axis=0, concat_axis=0, tiled=True)  40.4 us
    unnamed x128, local copies, waits for them, and re-layouts  29.3 us
    dot_general x4, matrix products, rows_back(): lax.dot_general(left, right, (((1,), (1,)), ((), ())), preferred_element_...  29.1 us
    all_to_all x1, waiting for transfers between devices, shards(): lax.all_to_all(tokens, 'dp', split_axis=0, concat_axis=0, tiled=True)  19.9 us
    dot_general x4, matrix products, rows_inner(): lax.dot_general(left, right, (((0,), (0,)), ((), ())), preferred_element_...  18.5 us
  transfers between devices with their start and end apart: 4, of which 2 were waited for; matrix products, arithmetic and copies ran while one was open for 10% of the time, Pallas kernels for 0%

commit v1 on v0

--- a/solution.py
+++ b/solution.py
@@ -292,7 +292,7 @@
     )
     result = returned[0]
     token_grad = returned[1]
-    summed = lax.psum(attn_grads + mlp_sums, ("dp", "group"))
+    summed = lax.psum(lax.psum(attn_grads + mlp_sums, "group"), "dp")
     return (
         result,
         token_grad,

time: 700 us -> 1550 us (2.21)
  waiting for transfers between devices: 363 us -> 1190 us
  blocking collectives: 106 us -> 136 us
    psum x1 -> x2, waiting for transfers between devices: 343 us -> 1170 us  [shards(): summed = lax.psum(lax.psum(attn_grads + mlp_sums, 'group'), 'dp')]
    all_to_all x1, blocking collectives: 40.4 us -> 59.2 us  [shards(): lax.all_to_all(back_out, 'dp', split_axis=0, concat_axis=0, tiled=True)]
    psum x1 -> x2, blocking collectives: 54.2 us -> 65.5 us  [shards(): summed = lax.psum(lax.psum(attn_grads + mlp_sums, 'group'), 'dp')]
  transfers between devices with their start and end apart: 4 -> 5, of which waited for: 2 -> 3; matrix products, arithmetic and copies ran while one was open for 10% -> 4% of each run, Pallas kernels for 0% -> 0%
where the time goes in v1:
time: 1550 us; the launch traced here: 1540 us
  waiting for transfers between devices  1190 us (77%)
  blocking collectives  136 us (9%)
  matrix products  100 us (6%)
  local copies, waits for them, and re-layouts  58.6 us (4%)
  other arithmetic  34 us (2%)
    psum x2, waiting for transfers between devices, shards(): summed = lax.psum(lax.psum(attn_grads + mlp_sums, 'group'), 'dp')  1170 us
    psum x2, blocking collectives, shards(): summed = lax.psum(lax.psum(attn_grads + mlp_sums, 'group'), 'dp')  65.5 us
    all_to_all x1, blocking collectives, shards(): lax.all_to_all(back_out, 'dp', split_axis=0, concat_axis=0, tiled=True)  59.2 us
  transfers between devices with their start and end apart: 5, of which 3 were waited for; matrix products, arithmetic and copies ran while one was open for 4% of the time, Pallas kernels for 0%

profile of v1, /device:TPU:0, one launch (start us, length us, event | category | flops | bytes accessed | tf_op | source)
XLA Modules:
  0.0 1543.5 jit_solution(14187627019302548678)
XLA Ops:
  8.1 11.8 all_to_all.29
  19.9 4.2 all-to-all-start.1
  27.4 19.9 %all-to-all-done.1 = bf16[4,160,768]{2,1,0:T(8,128)(2,1)} async-done(((bf16[4,160,768]{2,1,0:T(8,128)(2,1)}), bf16[4,160,768]{2,1,0:T(8,128)(2,1)}, u32[]{:S(2)}, u32[]{:S(2)}) %all-to-all-start.1) | async-done | bytes 983072 | tf_op jit(solution)/shard_map/all_to_all | solution.py:198
  47.4 4.3 all-to-all-start.3
  51.7 4.4 gather_fusion
  60.1 4.7 fusion.12
  64.8 4.3 copy.59
  72.6 3.7 fusion
  77.1 5.5 fusion.29
  82.6 4.9 gather_fusion.2
  90.6 5.5 fusion.44
  96.2 19.0 %convert_reduce_fusion = (f32[3072]{0:T(1024)}, bf16[512,3072]{1,0:T(8,128)(2,1)S(1)}, f32[512,3072]{1,0:T(8,128)}) fusion(f32[512,3072]{1,0:T(8,128)S(1)} %fusion.44, f32[3072]{0:T(1024)S(1)} %copy-done.31, bf16[512,768]{1,0:T(8,128)(2,1)S(1)} %copy-done.7, bf16[3072,768]{1,0:T(8,128)(2,1)S(1)} %bitcast.103), kind=kOutput, calls=%fused_computation.15 | convolution fusion | flops 2533880832 | bytes 21258240 | tf_op jit(solution)/shard_map/dot_general | solution.py:31
  126.5 9.0 fusion.26
  135.5 9.9 multiply_reduce_fusion
  145.4 7.1 multiply_convert_fusion
  159.8 5.6 fusion.43
  167.0 3.8 convert_reduce_fusion.1
  170.8 5.3 fusion.39
  176.1 5.4 fusion.52
  181.6 344.8 %all-reduce.7.cloned.1.call-done = (f32[768,2304]{1,0:T(8,128)}, f32[768,768]{1,0:T(8,128)}, f32[768,3072]{1,0:T(8,128)}, f32[3072,768]{1,0:T(8,128)}) async-done(((f32[768,2304]{1,0:T(8,128)}, f32[768,768]{1,0:T(8,128)}, f32[768,3072]{1,0:T(8,128)}, f32[3072,768]{1,0:T(8,128)}), (f32[768,2304]{1,0:T(8,128)}, f32[768,768]{1,0:T(8,128)}, f32[768,3072]{1,0:T(8,128)}, ...) | async-done | bytes 28311568 | tf_op jit(solution)/shard_map/psum | solution.py:295
  529.8 4.9 fusion.45
  538.2 5.2 gather_fusion.3
  543.4 7.2 add_convert_fusion.2
  550.6 5.2 gather_fusion.1
  558.4 59.2 %all_to_all.30 = bf16[4,160,768]{2,1,0:T(8,128)(2,1)} all-to-all(bf16[4,160,768]{2,1,0:T(8,128)(2,1)S(1)} %get-tuple-element.118), channel_id=1, replica_groups=mesh['dp'=4,'group'=8] {'dp'}, dimensions={0} | all-to-all | bytes 1966080 | tf_op jit(solution)/shard_map/all_to_all | solution.py:290
  617.6 4.2 all-to-all-start.4
  624.0 25.5 %all-reduce = (f32[768]{0:T(1024)}, f32[768]{0:T(1024)}, f32[2,768]{1,0:T(2,128)S(1)}, f32[768]{0:T(1024)}, f32[768]{0:T(1024)}, /*index=5*/f32[768]{0:T(1024)}, f32[3072]{0:T(1024)}, f32[768]{0:T(1024)}) all-reduce(f32[768]{0:T(1024)} %get-tuple-element.62, ...), channel_id=1, replica_groups=mesh['dp'=4,'group'=8] {'group'}, use_global_device_ids=true, to_apply=%region_15.16 | all-reduce | flops 9216 | bytes 73728 | tf_op jit(solution)/shard_map/psum | solution.py:295
  649.4 40.1 %all-reduce.2 = (f32[768]{0:T(1024)}, f32[768]{0:T(1024)}, f32[2,768]{1,0:T(2,128)}, f32[768]{0:T(1024)}, f32[768]{0:T(1024)}, /*index=5*/f32[768]{0:T(1024)}, f32[3072]{0:T(1024)}, f32[768]{0:T(1024)}) all-reduce(f32[768]{0:T(1024)} %get-tuple-element.80, f32[768]{0:T(1024)} %get-tuple-element.81, ...), channel_id=1, replica_groups=mesh['dp'=4,'group'=8] {'dp'}, use_global_device_ids=true, to_apply=%region_16.17 | all-reduce | flops 9216 | bytes 73728 | tf_op jit(solution)/shard_map/psum | solution.py:295
  689.5 821.3 %all-reduce.9.cloned.1.call-done = (f32[768,2304]{1,0:T(8,128)}, f32[768,768]{1,0:T(8,128)}, f32[768,3072]{1,0:T(8,128)}, f32[3072,768]{1,0:T(8,128)}) async-done(((f32[768,2304]{1,0:T(8,128)}, f32[768,768]{1,0:T(8,128)}, f32[768,3072]{1,0:T(8,128)}, f32[3072,768]{1,0:T(8,128)}), (f32[768,2304]{1,0:T(8,128)}, f32[768,768]{1,0:T(8,128)}, f32[768,3072]{1,0:T(8,128)}, ...) | async-done | bytes 28311568 | tf_op jit(solution)/shard_map/psum | solution.py:295
  1515.2 6.6 copy.81
  1523.2 9.3 copy.83
  1532.6 3.7 copy.84
  (185 shorter events, 53.2 us)
Async XLA Ops:
  7.2 52.9 %copy-start = (bf16[768,2304]{1,0:T(8,128)(2,1)S(1)}, bf16[768,2304]{1,0:T(8,128)(2,1)}, u32[]{:S(2)}) copy-start(bf16[768,2304]{1,0:T(8,128)(2,1)} %param.20) | copy-start | bytes 10616836
  19.9 27.5 %all-to-all-start.1 = ((bf16[4,160,768]{2,1,0:T(8,128)(2,1)}), bf16[4,160,768]{2,1,0:T(8,128)(2,1)}, u32[]{:S(2)}, u32[]{:S(2)}) async-start(bf16[4,160,768]{2,1,0:T(8,128)(2,1)} %param.15), calls=%async_computation.1 | async-start | bytes 1966080 | tf_op jit(solution)/shard_map/all_to_all | solution.py:198
  47.4 35.3 %all-to-all-start.3 = ((bf16[4,160,768]{2,1,0:T(8,128)(2,1)}), bf16[4,160,768]{2,1,0:T(8,128)(2,1)}, u32[]{:S(2)}, u32[]{:S(2)}) async-start(bf16[4,160,768]{2,1,0:T(8,128)(2,1)} %param.16), calls=%async_computation.3 | async-start | bytes 1966080 | tf_op jit(solution)/shard_map/all_to_all | solution.py:199
  51.6 8.5 copy-start.28
  51.6 8.5 copy-start.42
  51.7 474.7 %all-reduce.7.cloned.1.call-start = ((), (), s32[]{:S(2)}) async-start(), calls=%async_computation.5 | async-start | bytes 56623104 | tf_op jit(solution)/shard_map/psum | solution.py:295
  90.2 28.6 %copy-start.11 = (f32[512,768]{1,0:T(8,128)}, f32[512,768]{1,0:T(8,128)S(1)}, u32[]{:S(2)}) copy-start(f32[512,768]{1,0:T(8,128)S(1)} %get-tuple-element.122) | copy-start | bytes 4718596
  90.2 5.9 slice-start.12
  90.6 24.6 %slice-start.10 = ((s8[4718592]{0:T(1024)(128)(4,1)}), s8[4194304]{0:T(1024)(128)(4,1)S(1)}, s32[]{:S(2)}) async-start(s8[4718592]{0:T(1024)(128)(4,1)} %bitcast.100), calls=%async_computation.17 | async-start | bytes 8388608
  96.2 19.0 %copy-start.13 = (f32[512,3072]{1,0:T(8,128)}, f32[512,3072]{1,0:T(8,128)S(1)}, u32[]{:S(2)}) copy-start(f32[512,3072]{1,0:T(8,128)S(1)} %fusion.44) | copy-start | bytes 18874372
  96.2 19.0 %slice-start.11 = ((s8[4718592]{0:T(1024)(128)(4,1)}), s8[524288]{0:T(1024)(128)(4,1)S(1)}, s32[]{:S(2)}) async-start(s8[4718592]{0:T(1024)(128)(4,1)} %bitcast.100), calls=%async_computation.18 | async-start | bytes 1048576
  126.5 9.0 copy-start.10
  126.5 9.0 copy-start.14
  126.5 9.0 copy-start.21
  126.5 18.9 %slice-start = ((s8[12582912]{0:T(1024)(128)(4,1)}), s8[4194304]{0:T(1024)(128)(4,1)S(1)}, s32[]{:S(2)}) async-start(s8[12582912]{0:T(1024)(128)(4,1)} %bitcast.74), calls=%async_computation.7 | async-start | bytes 8388608
  126.5 18.9 %slice-start.1 = ((s8[12582912]{0:T(1024)(128)(4,1)}), s8[4194304]{0:T(1024)(128)(4,1)S(1)}, s32[]{:S(2)}) async-start(s8[12582912]{0:T(1024)(128)(4,1)} %bitcast.74), calls=%async_computation.8 | async-start | bytes 8388608
  135.5 9.9 slice-start.2
  145.4 7.2 copy-start.2
  157.5 7.8 slice-start.6
  157.5 7.8 slice-start.8
  159.7 5.6 slice-start.7
  159.7 5.6 slice-start.9
  159.7 5.6 copy-start.32
  166.9 9.2 copy-start.17
  181.6 1329.2 %all-reduce.9.cloned.1.call-start = ((), (), s32[]{:S(2)}) async-start(), calls=%async_computation.6 | async-start | bytes 56623104 | tf_op jit(solution)/shard_map/psum | solution.py:295
  529.8 6.2 copy-start.6
  529.8 6.2 copy-start.9
  617.6 71.9 %all-to-all-start.4 = ((bf16[4,160,768]{2,1,0:T(8,128)(2,1)}), bf16[4,160,768]{2,1,0:T(8,128)(2,1)}, u32[]{:S(2)}, u32[]{:S(2)}) async-start(bf16[4,160,768]{2,1,0:T(8,128)(2,1)} %get-tuple-element.117), calls=%async_computation.4 | async-start | bytes 1966080 | tf_op jit(solution)/shard_map/all_to_all | solution.py:291
  1515.2 6.6 copy-start.18
  1521.8 10.7 slice-start.3
  1523.2 9.3 slice-start.4
  1523.2 9.3 slice-start.5
  (34 other events, 122.2 us)
Sparse Core Ops, SparseCore 0:
  181.7 344.6 all-reduce.6
  529.3 981.4 all-reduce.8
